TPU v7x, 256 devices: a whole 4x4x8 slice. The times are simulated.
256 devices in a mesh: seq: 32 (over z, x_lo, core), dp: 8 (over y, x_hi).
Axes of the slice: x: 4 (x_hi: 2, x_lo: 2; x = x_hi * 2 + x_lo), y: 4, z: 8, core: 2. Of those that a mesh axis runs over, the one named last changes fastest.
Arguments:
- queries: bfloat16 [8, 4096, 2048], P('dp', 'seq'), may hold values from -18 to 18
- key_vectors: bfloat16 [8, 4096, 2048], P('dp', 'seq'), may hold values from -18 to 18
- value_vectors: bfloat16 [8, 4096, 2048], P('dp', 'seq'), may hold values from -6 to 6
- cotangent: bfloat16 [8, 4096, 2048], P('dp', 'seq'), may hold values from -6 to 6
- compress_kernel: bfloat16 [512, 128], replicated, may hold values from -0.25 to 0.25
- memory_reach: int32 [8, 32], P('dp', 'seq'), may hold values from 1 to 4, as said below
Outputs:
- attended: bfloat16 [8, 4096, 2048], P('dp', 'seq')
- grad_queries: bfloat16 [8, 4096, 2048], P('dp', 'seq')
- grad_keys: bfloat16 [8, 4096, 2048], P('dp', 'seq')
- grad_values: bfloat16 [8, 4096, 2048], P('dp', 'seq')
- grad_kernel: float32 [512, 128], P('seq')
Inputs may be any that keep to these rules, and one draw needn't show every extreme that they name: `memory_reach`: some segment reads 4 earlier segments and some reads 1.
All inputs are finite; a program needn't handle non-finite values.
Results may differ from a plain program's by a relative error of at most 0.0076.
Values may be sent and summed in bfloat16 or wider, within the bound.
A program may use at most 64 MiB of HBM per device.

v0:
```python
import jax
import jax.numpy as jnp
from jax import lax
from jax.sharding import PartitionSpec as P

H = 16
E = 128


def shifted(value, axis, steps):
    count = lax.axis_size(axis)
    initial, last = (max(0, -steps), min(count, count - steps))
    return lax.ppermute(value, axis, [(source, source + steps) for source in range(initial, last)])


def attend_block(query_rows, key_rows, value_rows, grad_rows, memory_keys, memory_values, visible):
    segment_len = query_rows.shape[0]
    slot_rows = segment_len // 4
    span_len = 2 * segment_len
    score_scale = E ** (-0.5)
    query_heads = query_rows.reshape(segment_len, H, E)
    grad_heads = grad_rows.reshape(segment_len, H, E)
    key_heads = jnp.concatenate([memory_keys, key_rows], 0).reshape(span_len, H, E)
    value_heads = jnp.concatenate([memory_values, value_rows], 0).reshape(span_len, H, E)
    columns = jnp.arange(span_len, dtype=jnp.int32)
    row_ids = jnp.arange(segment_len, dtype=jnp.int32)
    slot_of = jnp.minimum(columns // slot_rows, 3)
    memory_open = jnp.any(
        (slot_of[:, None] == jnp.arange(4, dtype=jnp.int32)[None, :]) & visible[None, :], axis=1
    )
    allowed = jnp.where(
        columns[None, :] < segment_len,
        memory_open[None, :],
        columns[None, :] - segment_len <= row_ids[:, None],
    )
    scores = (
        jnp.einsum("shd,lhd->hsl", query_heads, key_heads, preferred_element_type=jnp.float32)
        * score_scale
    )
    scores = jnp.where(allowed[None], scores, -1e30)
    highest = jnp.max(scores, axis=2, keepdims=True)
    raised = jnp.where(allowed[None], jnp.exp(scores - highest), 0.0)
    weights = raised / jnp.sum(raised, axis=2, keepdims=True)
    weights_low = weights.astype(jnp.bfloat16)
    attended = jnp.einsum(
        "hsl,lhd->shd", weights_low, value_heads, preferred_element_type=jnp.float32
    )
    grad_weights = jnp.einsum(
        "shd,lhd->hsl", grad_heads, value_heads, preferred_element_type=jnp.float32
    )
    row_delta = jnp.sum(weights * grad_weights, axis=2, keepdims=True)
    grad_scores = (weights * (grad_weights - row_delta) * score_scale).astype(jnp.bfloat16)
    grad_query = jnp.einsum(
        "hsl,lhd->shd", grad_scores, key_heads, preferred_element_type=jnp.float32
    )
    grad_key_list = jnp.einsum(
        "hsl,shd->lhd", grad_scores, query_heads, preferred_element_type=jnp.float32
    ).reshape(span_len, H * E)
    grad_value_list = jnp.einsum(
        "hsl,shd->lhd", weights_low, grad_heads, preferred_element_type=jnp.float32
    ).reshape(span_len, H * E)
    return (
        attended.reshape(segment_len, H * E).astype(jnp.bfloat16),
        grad_query.reshape(segment_len, H * E).astype(jnp.bfloat16),
        grad_key_list[segment_len:],
        grad_value_list[segment_len:],
        grad_key_list[:segment_len],
        grad_value_list[:segment_len],
    )


def local(queries, key_vectors, value_vectors, cotangent, compress_kernel, memory_reach):
    query_rows = queries[0]
    key_rows = key_vectors[0]
    value_rows = value_vectors[0]
    grad_rows = cotangent[0]
    segment_len = query_rows.shape[0]
    slot_rows = segment_len // 4
    kernel = compress_kernel.reshape(4, E, E)
    key_blocks = key_rows.reshape(slot_rows, 4, H, E)
    value_blocks = value_rows.reshape(slot_rows, 4, H, E)
    packed_keys = (
        jnp.einsum("mthe,tef->mhf", key_blocks, kernel, preferred_element_type=jnp.float32)
        .astype(jnp.bfloat16)
        .reshape(slot_rows, H * E)
    )
    packed_values = (
        jnp.einsum("mthe,tef->mhf", value_blocks, kernel, preferred_element_type=jnp.float32)
        .astype(jnp.bfloat16)
        .reshape(slot_rows, H * E)
    )
    received = []
    for offset in range(1, 5):
        received.append(shifted((packed_keys, packed_values), "seq", offset))
    memory_keys = jnp.concatenate([shifted_pair[0] for shifted_pair in received], 0)
    memory_values = jnp.concatenate([shifted_pair[1] for shifted_pair in received], 0)
    position = lax.axis_index("seq")
    slot_ids = jnp.arange(1, 5, dtype=jnp.int32)
    visible = (slot_ids <= memory_reach[0, 0]) & (position - slot_ids >= 0)
    attended, grad_query, local_keys, local_values, memory_grad_keys, memory_grad_values = (
        attend_block(
            query_rows, key_rows, value_rows, grad_rows, memory_keys, memory_values, visible
        )
    )
    slot_keys = memory_grad_keys.reshape(4, slot_rows, H * E)
    slot_values = memory_grad_values.reshape(4, slot_rows, H * E)
    summed_keys = jnp.zeros((slot_rows, H * E), jnp.float32)
    summed_values = jnp.zeros((slot_rows, H * E), jnp.float32)
    for offset in range(1, 5):
        arrived = shifted((slot_keys[offset - 1], slot_values[offset - 1]), "seq", -offset)
        summed_keys = summed_keys + arrived[0]
        summed_values = summed_values + arrived[1]
    packed_grad_keys = summed_keys.astype(jnp.bfloat16).reshape(slot_rows, H, E)
    packed_grad_values = summed_values.astype(jnp.bfloat16).reshape(slot_rows, H, E)
    back_keys = jnp.einsum(
        "mhf,tef->mthe", packed_grad_keys, kernel, preferred_element_type=jnp.float32
    ).reshape(segment_len, H * E)
    back_values = jnp.einsum(
        "mhf,tef->mthe", packed_grad_values, kernel, preferred_element_type=jnp.float32
    ).reshape(segment_len, H * E)
    key_grad = (local_keys + back_keys).astype(jnp.bfloat16)
    value_grad = (local_values + back_values).astype(jnp.bfloat16)
    kernel_terms = (
        jnp.einsum(
            "mthe,mhf->tef", key_blocks, packed_grad_keys, preferred_element_type=jnp.float32
        )
        + jnp.einsum(
            "mthe,mhf->tef", value_blocks, packed_grad_values, preferred_element_type=jnp.float32
        )
    ).reshape(4 * E, E)
    whole_sum = lax.psum(kernel_terms, ("seq", "dp"))
    share_rows = 4 * E // lax.axis_size("seq")
    grad_kernel = lax.dynamic_slice_in_dim(
        whole_sum, lax.axis_index("seq") * share_rows, share_rows, 0
    )
    return (attended[None], grad_query[None], key_grad[None], value_grad[None], grad_kernel)


def solution(mesh):
    return jax.shard_map(
        local,
        mesh=mesh,
        in_specs=(
            P("dp", "seq", None),
            P("dp", "seq", None),
            P("dp", "seq", None),
            P("dp", "seq", None),
            P(),
            P("dp", "seq"),
        ),
        out_specs=(
            P("dp", "seq", None),
            P("dp", "seq", None),
            P("dp", "seq", None),
            P("dp", "seq", None),
            P("seq", None),
        ),
        check_vma=False,
    )
```

profile of v0, /device:TPU:2, one launch (start us, length us, event | category | flops | bytes accessed | tf_op | source)
XLA Modules:
  0.0 406.7 jit_solution(10729442592492152735)
XLA Ops:
  9.5 3.8 collective-permute-start.3
  13.3 3.0 collective-permute-start.2
  16.2 3.4 collective-permute-start.1
  19.7 3.0 collective-permute-start
  23.8 2.8 collective-permute-start.4
  31.6 3.4 collective-permute-start.5
  35.9 3.9 collective-permute-done.5
  39.8 4.0 collective-permute-start.6
  43.8 3.7 collective-permute-done.6
  47.5 4.7 %collective-permute-start.7 = (bf16[32,2048]{1,0:T(8,128)(2,1)}, bf16[32,2048]{1,0:T(8,128)(2,1)S(1)}, u32[]{:S(2)}, u32[]{:S(2)}) collective-permute-start(bf16[32,2048]{1,0:T(8,128)(2,1)} %bitcast.201), channel_id=1, source_target_pairs={{0,32},{8,40},{16,48},{24,56},{32,64},{40,72},{48,80},{56,88},{64,... | collective-permute-start | bytes 393224 | tf_op jit(solution)/shard_map/ppermute | solution.py:13
  52.3 2.8 collective-permute-done.7
  61.5 2.8 concatenate.33
  64.3 2.9 fusion.18
  67.2 3.5 fusion.45
  70.7 3.0 convolution_convert_fusion.1
  74.2 6.5 %convolution_bitcast_fusion.1 = f32[256,16,128]{2,0,1:T(8,128)} fusion(f32[16,256,128]{2,1,0:T(8,128)} %fusion.18, bf16[128,16,128]{2,1,0:T(8,128)(2,1)} %bitcast.229, f32[16,128,256]{1,2,0:T(8,128)} %get-tuple-element.29, f32[16,128]{1,0:T(8,128)S(1)} %get-tuple-element.28), kind=kOutput, calls=%fused_computation.11 | convolution fusion | flops 137890048 | bytes 6823936 | tf_op jit(solution)/shard_map/hsl,shd->lhd/dot_general | solution.py:56
  90.1 5.6 %convolution_convert_fusion = bf16[16,128,128]{2,1,0:T(8,128)(2,1)} fusion(bf16[256,16,128]{2,0,1:T(8,128)(2,1)} %constant_dynamic-update-slice_fusion, f32[16,256,128]{2,1,0:T(8,128)} %fusion.18, f32[16,128,256]{1,2,0:T(8,128)} %get-tuple-element.29, f32[16,128]{1,0:T(8,128)S(1)} %get-tuple-element.28), kind=kOutput, calls=%fused_computation.14 | convolution fusion | flops 138152192 | bytes 5775360 | tf_op jit(solution)/shard_map/hsl,lhd->shd/dot_general | solution.py:53
  95.6 2.1 copy.102
  118.1 2.5 copy.99
  121.0 2.6 collective-permute-done.10
  123.6 3.7 collective-permute-done.11
  127.3 8.5 %collective-permute-done.9 = f32[32,2048]{1,0:T(8,128)} collective-permute-done((f32[32,2048]{1,0:T(8,128)}, f32[32,2048]{1,0:T(8,128)}, u32[]{:S(2)}, u32[]{:S(2)}) %collective-permute-start.9) | collective-permute-done | bytes 262176 | tf_op jit(solution)/shard_map/ppermute | solution.py:13
  139.6 2.7 copy.92
  146.8 251.8 %all-reduce.2.cloned.1.call-done = f32[512,128]{1,0:T(8,128)} async-done(((f32[512,128]{1,0:T(8,128)}), f32[512,128]{1,0:T(8,128)}) %all-reduce.2.cloned.1.call-update) | async-done | bytes 262160 | tf_op jit(solution)/shard_map/psum | solution.py:131
  (111 shorter events, 55.0 us)
Async XLA Ops:
  7.2 15.5 %copy-start.8 = (bf16[1,128,2048]{2,1,0:T(8,128)(2,1)S(1)}, bf16[1,128,2048]{2,1,0:T(8,128)(2,1)}, u32[]{:S(2)}) copy-start(bf16[1,128,2048]{2,1,0:T(8,128)(2,1)} %param.7) | copy-start | bytes 1572868
  7.2 391.3 %all-reduce.2.cloned.1.call-start = ((), (), s32[]{:S(2)}) async-start(), calls=%async_computation | async-start | bytes 524288 | tf_op jit(solution)/shard_map/psum | solution.py:131
  8.5 18.5 %copy-start.9 = (bf16[1,128,2048]{2,1,0:T(8,128)(2,1)S(1)}, bf16[1,128,2048]{2,1,0:T(8,128)(2,1)}, u32[]{:S(2)}) copy-start(bf16[1,128,2048]{2,1,0:T(8,128)(2,1)} %param.8) | copy-start | bytes 1572868
  9.5 51.0 %collective-permute-start.3 = (bf16[32,2048]{1,0:T(8,128)(2,1)}, bf16[32,2048]{1,0:T(8,128)(2,1)S(1)}, u32[]{:S(2)}, u32[]{:S(2)}) collective-permute-start(bf16[32,2048]{1,0:T(8,128)(2,1)} %bitcast.202), channel_id=1, source_target_pairs={{0,32},{8,40},{16,48},{24,56},{32,64},{40,72},{48,80},{56,88},{64,... | collective-permute-start | bytes 393224 | tf_op jit(solution)/shard_map/ppermute | solution.py:13
  13.3 45.3 %collective-permute-start.2 = (bf16[32,2048]{1,0:T(8,128)(2,1)}, bf16[32,2048]{1,0:T(8,128)(2,1)S(1)}, u32[]{:S(2)}, u32[]{:S(2)}) collective-permute-start(bf16[32,2048]{1,0:T(8,128)(2,1)} %bitcast.202), channel_id=1, source_target_pairs={{0,24},{8,32},{16,40},{24,48},{32,56},{40,64},{48,72},{56,80},{64,... | collective-permute-start | bytes 393224 | tf_op jit(solution)/shard_map/ppermute | solution.py:13
  16.2 41.1 %collective-permute-start.1 = (bf16[32,2048]{1,0:T(8,128)(2,1)}, bf16[32,2048]{1,0:T(8,128)(2,1)}, u32[]{:S(2)}, u32[]{:S(2)}) collective-permute-start(bf16[32,2048]{1,0:T(8,128)(2,1)} %bitcast.202), channel_id=1, source_target_pairs={{0,16},{8,24},{16,32},{24,40},{32,48},{40,56},{48,64},{56,72},{64,... | collective-permute-start | bytes 393224 | tf_op jit(solution)/shard_map/ppermute | solution.py:13
  19.7 36.5 %collective-permute-start = (bf16[32,2048]{1,0:T(8,128)(2,1)}, bf16[32,2048]{1,0:T(8,128)(2,1)}, u32[]{:S(2)}, u32[]{:S(2)}) collective-permute-start(bf16[32,2048]{1,0:T(8,128)(2,1)} %bitcast.202), channel_id=1, source_target_pairs={{0,8},{8,16},{16,24},{24,32},{32,40},{40,48},{48,56},{56,64},{64,7... | collective-permute-start | bytes 393224 | tf_op jit(solution)/shard_map/ppermute | solution.py:13
  22.7 5.9 %copy-start.10 = (bf16[1,128,2048]{2,1,0:T(8,128)(2,1)S(1)}, bf16[1,128,2048]{2,1,0:T(8,128)(2,1)}, u32[]{:S(2)}) copy-start(bf16[1,128,2048]{2,1,0:T(8,128)(2,1)} %param.6) | copy-start | bytes 1572868
  23.8 7.8 %collective-permute-start.4 = (bf16[32,2048]{1,0:T(8,128)(2,1)}, bf16[32,2048]{1,0:T(8,128)(2,1)}, u32[]{:S(2)}, u32[]{:S(2)}) collective-permute-start(bf16[32,2048]{1,0:T(8,128)(2,1)} %bitcast.201), channel_id=1, source_target_pairs={{0,8},{8,16},{16,24},{24,32},{32,40},{40,48},{48,56},{56,64},{64,7... | collective-permute-start | bytes 393224 | tf_op jit(solution)/shard_map/ppermute | solution.py:13
  31.6 8.2 %collective-permute-start.5 = (bf16[32,2048]{1,0:T(8,128)(2,1)}, bf16[32,2048]{1,0:T(8,128)(2,1)S(1)}, u32[]{:S(2)}, u32[]{:S(2)}) collective-permute-start(bf16[32,2048]{1,0:T(8,128)(2,1)} %bitcast.201), channel_id=1, source_target_pairs={{0,16},{8,24},{16,32},{24,40},{32,48},{40,56},{48,64},{56,72},{64,... | collective-permute-start | bytes 393224 | tf_op jit(solution)/shard_map/ppermute | solution.py:13
  39.8 7.7 %collective-permute-start.6 = (bf16[32,2048]{1,0:T(8,128)(2,1)}, bf16[32,2048]{1,0:T(8,128)(2,1)S(1)}, u32[]{:S(2)}, u32[]{:S(2)}) collective-permute-start(bf16[32,2048]{1,0:T(8,128)(2,1)} %bitcast.201), channel_id=1, source_target_pairs={{0,24},{8,32},{16,40},{24,48},{32,56},{40,64},{48,72},{56,80},{64,... | collective-permute-start | bytes 393224 | tf_op jit(solution)/shard_map/ppermute | solution.py:13
  47.5 7.6 %collective-permute-start.7 = (bf16[32,2048]{1,0:T(8,128)(2,1)}, bf16[32,2048]{1,0:T(8,128)(2,1)S(1)}, u32[]{:S(2)}, u32[]{:S(2)}) collective-permute-start(bf16[32,2048]{1,0:T(8,128)(2,1)} %bitcast.201), channel_id=1, source_target_pairs={{0,32},{8,40},{16,48},{24,56},{32,64},{40,72},{48,80},{56,88},{64,... | collective-permute-start | bytes 393224 | tf_op jit(solution)/shard_map/ppermute | solution.py:13
  74.2 21.5 %copy-start.4 = (f32[256,16,128]{2,0,1:T(8,128)}, f32[256,16,128]{2,0,1:T(8,128)S(1)}, u32[]{:S(2)}) copy-start(f32[256,16,128]{2,0,1:T(8,128)S(1)} %convolution_bitcast_fusion) | copy-start | bytes 6291460
  83.6 27.0 %collective-permute-start.12 = (f32[32,2048]{1,0:T(8,128)}, f32[32,2048]{1,0:T(8,128)}, u32[]{:S(2)}, u32[]{:S(2)}) collective-permute-start(f32[32,2048]{1,0:T(8,128)} %bitcast.196), channel_id=1, source_target_pairs={{8,0},{16,8},{24,16},{32,24},{40,32},{48,40},{56,48},{64,56},{72,6... | collective-permute-start | bytes 786440 | tf_op jit(solution)/shard_map/ppermute | solution.py:13
  85.5 26.4 %collective-permute-start.14 = (f32[32,2048]{1,0:T(8,128)}, f32[32,2048]{1,0:T(8,128)}, u32[]{:S(2)}, u32[]{:S(2)}) collective-permute-start(f32[32,2048]{1,0:T(8,128)} %bitcast.194), channel_id=1, source_target_pairs={{24,0},{32,8},{40,16},{48,24},{56,32},{64,40},{72,48},{80,56},{88,... | collective-permute-start | bytes 786440 | tf_op jit(solution)/shard_map/ppermute | solution.py:13
  86.8 26.4 %collective-permute-start.15 = (f32[32,2048]{1,0:T(8,128)}, f32[32,2048]{1,0:T(8,128)}, u32[]{:S(2)}, u32[]{:S(2)}) collective-permute-start(f32[32,2048]{1,0:T(8,128)} %bitcast.193), channel_id=1, source_target_pairs={{32,0},{40,8},{48,16},{56,24},{64,32},{72,40},{80,48},{88,56},{96,... | collective-permute-start | bytes 786440 | tf_op jit(solution)/shard_map/ppermute | solution.py:13
  88.1 27.2 %collective-permute-start.13 = (f32[32,2048]{1,0:T(8,128)}, f32[32,2048]{1,0:T(8,128)}, u32[]{:S(2)}, u32[]{:S(2)}) collective-permute-start(f32[32,2048]{1,0:T(8,128)} %bitcast.195), channel_id=1, source_target_pairs={{16,0},{24,8},{32,16},{40,24},{48,32},{56,40},{64,48},{72,56},{80,... | collective-permute-start | bytes 786440 | tf_op jit(solution)/shard_map/ppermute | solution.py:13
  95.6 4.2 %slice-start.1 = ((f32[256,16,128]{2,0,1:T(8,128)}), f32[128,16,128]{2,0,1:T(8,128)S(1)}, s32[]{:S(2)}) async-start(f32[256,16,128]{2,0,1:T(8,128)} %copy-done.4), calls=%async_computation.2 | async-start | bytes 2097152 | tf_op jit(solution)/shard_map/slice | solution.py:66
  100.2 3.2 slice-start
  108.7 12.3 %collective-permute-start.8 = (f32[32,2048]{1,0:T(8,128)}, f32[32,2048]{1,0:T(8,128)}, u32[]{:S(2)}, u32[]{:S(2)}) collective-permute-start(f32[32,2048]{1,0:T(8,128)} %bitcast.200), channel_id=1, source_target_pairs={{8,0},{16,8},{24,16},{32,24},{40,32},{48,40},{56,48},{64,56},{72,6... | collective-permute-start | bytes 786440 | tf_op jit(solution)/shard_map/ppermute | solution.py:13
  110.6 13.0 %collective-permute-start.10 = (f32[32,2048]{1,0:T(8,128)}, f32[32,2048]{1,0:T(8,128)}, u32[]{:S(2)}, u32[]{:S(2)}) collective-permute-start(f32[32,2048]{1,0:T(8,128)} %bitcast.198), channel_id=1, source_target_pairs={{24,0},{32,8},{40,16},{48,24},{56,32},{64,40},{72,48},{80,56},{88,... | collective-permute-start | bytes 786440 | tf_op jit(solution)/shard_map/ppermute | solution.py:13
  112.0 15.3 %collective-permute-start.11 = (f32[32,2048]{1,0:T(8,128)}, f32[32,2048]{1,0:T(8,128)}, u32[]{:S(2)}, u32[]{:S(2)}) collective-permute-start(f32[32,2048]{1,0:T(8,128)} %bitcast.197), channel_id=1, source_target_pairs={{32,0},{40,8},{48,16},{56,24},{64,32},{72,40},{80,48},{88,56},{96,... | collective-permute-start | bytes 786440 | tf_op jit(solution)/shard_map/ppermute | solution.py:13
  113.3 22.5 %collective-permute-start.9 = (f32[32,2048]{1,0:T(8,128)}, f32[32,2048]{1,0:T(8,128)}, u32[]{:S(2)}, u32[]{:S(2)}) collective-permute-start(f32[32,2048]{1,0:T(8,128)} %bitcast.235), channel_id=1, source_target_pairs={{16,0},{24,8},{32,16},{40,24},{48,32},{56,40},{64,48},{72,56},{80,... | collective-permute-start | bytes 786440 | tf_op jit(solution)/shard_map/ppermute | solution.py:13
  139.6 3.6 copy-start.1
  (11 other events, 23.5 us)
Sparse Core Ops, SparseCore 0:
  138.6 259.9 all-reduce.1
where the time goes:
time: 408 us; the launch traced here: 407 us
  waiting for transfers between devices  277 us (68%)
  local copies, waits for them, and re-layouts  44.6 us (11%)
  starting transfers between devices  41.2 us (10%)
  matrix products  24.5 us (6%)
  between operations  15.2 us (4%)
  other arithmetic  4.38 us (1%)
    psum x1, waiting for transfers between devices, local(): whole_sum = lax.psum(kernel_terms, ('seq', 'dp'))  252 us
    ppermute x16, starting transfers between devices, shifted(): lax.ppermute(value, axis, [(source, source + steps) for source in range(i...  41.1 us
    ppermute x16, waiting for transfers between devices, shifted(): lax.ppermute(value, axis, [(source, source + steps) for source in range(i...  25.1 us
    unnamed x52, local copies, waits for them, and re-layouts  18.1 us
  transfers between devices with their start and end apart: 17, of which 7 were waited for; matrix products, arithmetic and copies ran while one was open for 10% of the time, Pallas kernels for 0%

commit v1 on v0

--- a/solution.py
+++ b/solution.py
@@ -128,7 +128,7 @@
             "mthe,mhf->tef", value_blocks, packed_grad_values, preferred_element_type=jnp.float32
         )
     ).reshape(4 * E, E)
-    whole_sum = lax.psum(kernel_terms, ("seq", "dp"))
+    whole_sum = lax.psum(lax.psum(kernel_terms, "seq"), axis_name="dp")
     share_rows = 4 * E // lax.axis_size("seq")
     grad_kernel = lax.dynamic_slice_in_dim(
         whole_sum, lax.axis_index("seq") * share_rows, share_rows, 0

time: 408 us -> 473 us (1.16)
  waiting for transfers between devices: 277 us -> 346 us
    psum x1 -> x2, waiting for transfers between devices: 252 us -> 321 us  [local(): whole_sum = lax.psum(lax.psum(kernel_terms, 'seq'), axis_name='dp')]
    unnamed x52 -> x46, local copies, waits for them, and re-layouts: 18.1 us -> 15.5 us
  transfers between devices with their start and end apart: 17 -> 18, of which waited for: 7 -> 8; matrix products, arithmetic and copies ran while one was open for 10% -> 8% of each run, Pallas kernels for 0% -> 0%
where the time goes in v1:
time: 473 us; the launch traced here: 471 us
  waiting for transfers between devices  346 us (73%)
  starting transfers between devices  41 us (9%)
  local copies, waits for them, and re-layouts  40.1 us (8%)
  matrix products  24.5 us (5%)
  between operations  15.2 us (3%)
  other arithmetic  4.8 us (1%)
    psum x2, waiting for transfers between devices, local(): whole_sum = lax.psum(lax.psum(kernel_terms, 'seq'), axis_name='dp')  321 us
    ppermute x16, starting transfers between devices, shifted(): lax.ppermute(value, axis, [(source, source + steps) for source in range(i...  40.9 us
    ppermute x16, waiting for transfers between devices, shifted(): lax.ppermute(value, axis, [(source, source + steps) for source in range(i...  25.3 us
    unnamed x46, local copies, waits for them, and re-layouts  15.5 us
  transfers between devices with their start and end apart: 18, of which 8 were waited for; matrix products, arithmetic and copies ran while one was open for 8% of the time, Pallas kernels for 0%

profile of v1, /device:TPU:2, one launch (start us, length us, event | category | flops | bytes accessed | tf_op | source)
XLA Modules:
  0.0 471.4 jit_solution(17341328246579317476)
XLA Ops:
  9.5 3.8 collective-permute-start.3
  13.3 3.0 collective-permute-start.2
  16.2 3.4 collective-permute-start.1
  19.6 3.0 collective-permute-start
  23.8 2.8 collective-permute-start.4
  31.6 3.4 collective-permute-start.5
  35.9 3.9 collective-permute-done.5
  39.8 4.0 collective-permute-start.6
  43.8 3.7 collective-permute-done.6
  47.5 4.7 %collective-permute-start.7 = (bf16[32,2048]{1,0:T(8,128)(2,1)}, bf16[32,2048]{1,0:T(8,128)(2,1)S(1)}, u32[]{:S(2)}, u32[]{:S(2)}) collective-permute-start(bf16[32,2048]{1,0:T(8,128)(2,1)} %bitcast.201), channel_id=1, source_target_pairs={{0,32},{8,40},{16,48},{24,56},{32,64},{40,72},{48,80},{56,88},{64,... | collective-permute-start | bytes 393224 | tf_op jit(solution)/shard_map/ppermute | solution.py:13
  52.3 2.8 collective-permute-done.7
  61.5 2.8 concatenate.33
  64.3 2.9 fusion.18
  67.2 3.5 fusion.45
  70.7 3.0 convolution_convert_fusion.1
  74.2 6.5 %convolution_bitcast_fusion.1 = f32[256,16,128]{2,0,1:T(8,128)} fusion(f32[16,256,128]{2,1,0:T(8,128)} %fusion.18, bf16[128,16,128]{2,1,0:T(8,128)(2,1)} %bitcast.229, f32[16,128,256]{1,2,0:T(8,128)} %get-tuple-element.29, f32[16,128]{1,0:T(8,128)S(1)} %get-tuple-element.28), kind=kOutput, calls=%fused_computation.11 | convolution fusion | flops 137890048 | bytes 6823936 | tf_op jit(solution)/shard_map/hsl,shd->lhd/dot_general | solution.py:56
  90.1 5.6 %convolution_convert_fusion = bf16[16,128,128]{2,1,0:T(8,128)(2,1)} fusion(bf16[256,16,128]{2,0,1:T(8,128)(2,1)} %constant_dynamic-update-slice_fusion, f32[16,256,128]{2,1,0:T(8,128)} %fusion.18, f32[16,128,256]{1,2,0:T(8,128)} %get-tuple-element.29, f32[16,128]{1,0:T(8,128)S(1)} %get-tuple-element.28), kind=kOutput, calls=%fused_computation.14 | convolution fusion | flops 138152192 | bytes 5775360 | tf_op jit(solution)/shard_map/hsl,lhd->shd/dot_general | solution.py:53
  95.6 2.1 copy.102
  118.2 2.5 copy.99
  121.1 2.8 collective-permute-done.10
  123.9 3.7 collective-permute-done.11
  127.6 8.5 %collective-permute-done.9 = f32[32,2048]{1,0:T(8,128)} collective-permute-done((f32[32,2048]{1,0:T(8,128)}, f32[32,2048]{1,0:T(8,128)}, u32[]{:S(2)}, u32[]{:S(2)}) %collective-permute-start.9) | collective-permute-done | bytes 262176 | tf_op jit(solution)/shard_map/ppermute | solution.py:13
  141.6 226.0 %all-reduce.3.cloned.1.call-done = f32[512,128]{1,0:T(8,128)} async-done(((f32[512,128]{1,0:T(8,128)}), f32[512,128]{1,0:T(8,128)}) %all-reduce.3.cloned.1.call-update) | async-done | bytes 262160 | tf_op jit(solution)/shard_map/psum | solution.py:131
  368.7 94.6 %all-reduce.5.cloned.1.call-done = f32[512,128]{1,0:T(8,128)} async-done(((f32[512,128]{1,0:T(8,128)}), f32[512,128]{1,0:T(8,128)}) %all-reduce.5.cloned.1.call-update) | async-done | bytes 262160 | tf_op jit(solution)/shard_map/psum | solution.py:131
  (107 shorter events, 53.4 us)
Async XLA Ops:
  7.2 15.5 %copy-start.5 = (bf16[1,128,2048]{2,1,0:T(8,128)(2,1)S(1)}, bf16[1,128,2048]{2,1,0:T(8,128)(2,1)}, u32[]{:S(2)}) copy-start(bf16[1,128,2048]{2,1,0:T(8,128)(2,1)} %param.7) | copy-start | bytes 1572868
  7.2 360.4 %all-reduce.3.cloned.1.call-start = ((), (), s32[]{:S(2)}) async-start(), calls=%async_computation | async-start | bytes 524288 | tf_op jit(solution)/shard_map/psum | solution.py:131
  8.5 18.5 %copy-start.6 = (bf16[1,128,2048]{2,1,0:T(8,128)(2,1)S(1)}, bf16[1,128,2048]{2,1,0:T(8,128)(2,1)}, u32[]{:S(2)}) copy-start(bf16[1,128,2048]{2,1,0:T(8,128)(2,1)} %param.8) | copy-start | bytes 1572868
  9.5 51.0 %collective-permute-start.3 = (bf16[32,2048]{1,0:T(8,128)(2,1)}, bf16[32,2048]{1,0:T(8,128)(2,1)S(1)}, u32[]{:S(2)}, u32[]{:S(2)}) collective-permute-start(bf16[32,2048]{1,0:T(8,128)(2,1)} %bitcast.202), channel_id=1, source_target_pairs={{0,32},{8,40},{16,48},{24,56},{32,64},{40,72},{48,80},{56,88},{64,... | collective-permute-start | bytes 393224 | tf_op jit(solution)/shard_map/ppermute | solution.py:13
  13.3 45.2 %collective-permute-start.2 = (bf16[32,2048]{1,0:T(8,128)(2,1)}, bf16[32,2048]{1,0:T(8,128)(2,1)S(1)}, u32[]{:S(2)}, u32[]{:S(2)}) collective-permute-start(bf16[32,2048]{1,0:T(8,128)(2,1)} %bitcast.202), channel_id=1, source_target_pairs={{0,24},{8,32},{16,40},{24,48},{32,56},{40,64},{48,72},{56,80},{64,... | collective-permute-start | bytes 393224 | tf_op jit(solution)/shard_map/ppermute | solution.py:13
  16.2 41.1 %collective-permute-start.1 = (bf16[32,2048]{1,0:T(8,128)(2,1)}, bf16[32,2048]{1,0:T(8,128)(2,1)}, u32[]{:S(2)}, u32[]{:S(2)}) collective-permute-start(bf16[32,2048]{1,0:T(8,128)(2,1)} %bitcast.202), channel_id=1, source_target_pairs={{0,16},{8,24},{16,32},{24,40},{32,48},{40,56},{48,64},{56,72},{64,... | collective-permute-start | bytes 393224 | tf_op jit(solution)/shard_map/ppermute | solution.py:13
  19.6 36.5 %collective-permute-start = (bf16[32,2048]{1,0:T(8,128)(2,1)}, bf16[32,2048]{1,0:T(8,128)(2,1)}, u32[]{:S(2)}, u32[]{:S(2)}) collective-permute-start(bf16[32,2048]{1,0:T(8,128)(2,1)} %bitcast.202), channel_id=1, source_target_pairs={{0,8},{8,16},{16,24},{24,32},{32,40},{40,48},{48,56},{56,64},{64,7... | collective-permute-start | bytes 393224 | tf_op jit(solution)/shard_map/ppermute | solution.py:13
  22.7 5.9 %copy-start.7 = (bf16[1,128,2048]{2,1,0:T(8,128)(2,1)S(1)}, bf16[1,128,2048]{2,1,0:T(8,128)(2,1)}, u32[]{:S(2)}) copy-start(bf16[1,128,2048]{2,1,0:T(8,128)(2,1)} %param.6) | copy-start | bytes 1572868
  23.8 7.8 %collective-permute-start.4 = (bf16[32,2048]{1,0:T(8,128)(2,1)}, bf16[32,2048]{1,0:T(8,128)(2,1)}, u32[]{:S(2)}, u32[]{:S(2)}) collective-permute-start(bf16[32,2048]{1,0:T(8,128)(2,1)} %bitcast.201), channel_id=1, source_target_pairs={{0,8},{8,16},{16,24},{24,32},{32,40},{40,48},{48,56},{56,64},{64,7... | collective-permute-start | bytes 393224 | tf_op jit(solution)/shard_map/ppermute | solution.py:13
  31.6 8.2 %collective-permute-start.5 = (bf16[32,2048]{1,0:T(8,128)(2,1)}, bf16[32,2048]{1,0:T(8,128)(2,1)S(1)}, u32[]{:S(2)}, u32[]{:S(2)}) collective-permute-start(bf16[32,2048]{1,0:T(8,128)(2,1)} %bitcast.201), channel_id=1, source_target_pairs={{0,16},{8,24},{16,32},{24,40},{32,48},{40,56},{48,64},{56,72},{64,... | collective-permute-start | bytes 393224 | tf_op jit(solution)/shard_map/ppermute | solution.py:13
  39.8 7.7 %collective-permute-start.6 = (bf16[32,2048]{1,0:T(8,128)(2,1)}, bf16[32,2048]{1,0:T(8,128)(2,1)S(1)}, u32[]{:S(2)}, u32[]{:S(2)}) collective-permute-start(bf16[32,2048]{1,0:T(8,128)(2,1)} %bitcast.201), channel_id=1, source_target_pairs={{0,24},{8,32},{16,40},{24,48},{32,56},{40,64},{48,72},{56,80},{64,... | collective-permute-start | bytes 393224 | tf_op jit(solution)/shard_map/ppermute | solution.py:13
  47.5 7.6 %collective-permute-start.7 = (bf16[32,2048]{1,0:T(8,128)(2,1)}, bf16[32,2048]{1,0:T(8,128)(2,1)S(1)}, u32[]{:S(2)}, u32[]{:S(2)}) collective-permute-start(bf16[32,2048]{1,0:T(8,128)(2,1)} %bitcast.201), channel_id=1, source_target_pairs={{0,32},{8,40},{16,48},{24,56},{32,64},{40,72},{48,80},{56,88},{64,... | collective-permute-start | bytes 393224 | tf_op jit(solution)/shard_map/ppermute | solution.py:13
  74.2 21.5 %copy-start.2 = (f32[256,16,128]{2,0,1:T(8,128)}, f32[256,16,128]{2,0,1:T(8,128)S(1)}, u32[]{:S(2)}) copy-start(f32[256,16,128]{2,0,1:T(8,128)S(1)} %convolution_bitcast_fusion) | copy-start | bytes 6291460
  83.6 27.3 %collective-permute-start.12 = (f32[32,2048]{1,0:T(8,128)}, f32[32,2048]{1,0:T(8,128)}, u32[]{:S(2)}, u32[]{:S(2)}) collective-permute-start(f32[32,2048]{1,0:T(8,128)} %bitcast.196), channel_id=1, source_target_pairs={{8,0},{16,8},{24,16},{32,24},{40,32},{48,40},{56,48},{64,56},{72,6... | collective-permute-start | bytes 786440 | tf_op jit(solution)/shard_map/ppermute | solution.py:13
  85.5 26.7 %collective-permute-start.14 = (f32[32,2048]{1,0:T(8,128)}, f32[32,2048]{1,0:T(8,128)}, u32[]{:S(2)}, u32[]{:S(2)}) collective-permute-start(f32[32,2048]{1,0:T(8,128)} %bitcast.194), channel_id=1, source_target_pairs={{24,0},{32,8},{40,16},{48,24},{56,32},{64,40},{72,48},{80,56},{88,... | collective-permute-start | bytes 786440 | tf_op jit(solution)/shard_map/ppermute | solution.py:13
  86.8 26.7 %collective-permute-start.15 = (f32[32,2048]{1,0:T(8,128)}, f32[32,2048]{1,0:T(8,128)}, u32[]{:S(2)}, u32[]{:S(2)}) collective-permute-start(f32[32,2048]{1,0:T(8,128)} %bitcast.193), channel_id=1, source_target_pairs={{32,0},{40,8},{48,16},{56,24},{64,32},{72,40},{80,48},{88,56},{96,... | collective-permute-start | bytes 786440 | tf_op jit(solution)/shard_map/ppermute | solution.py:13
  88.1 27.4 %collective-permute-start.13 = (f32[32,2048]{1,0:T(8,128)}, f32[32,2048]{1,0:T(8,128)}, u32[]{:S(2)}, u32[]{:S(2)}) collective-permute-start(f32[32,2048]{1,0:T(8,128)} %bitcast.195), channel_id=1, source_target_pairs={{16,0},{24,8},{32,16},{40,24},{48,32},{56,40},{64,48},{72,56},{80,... | collective-permute-start | bytes 786440 | tf_op jit(solution)/shard_map/ppermute | solution.py:13
  95.6 4.2 slice-start
  109.0 12.1 %collective-permute-start.8 = (f32[32,2048]{1,0:T(8,128)}, f32[32,2048]{1,0:T(8,128)}, u32[]{:S(2)}, u32[]{:S(2)}) collective-permute-start(f32[32,2048]{1,0:T(8,128)} %bitcast.200), channel_id=1, source_target_pairs={{8,0},{16,8},{24,16},{32,24},{40,32},{48,40},{56,48},{64,56},{72,6... | collective-permute-start | bytes 786440 | tf_op jit(solution)/shard_map/ppermute | solution.py:13
  111.0 13.0 %collective-permute-start.10 = (f32[32,2048]{1,0:T(8,128)}, f32[32,2048]{1,0:T(8,128)}, u32[]{:S(2)}, u32[]{:S(2)}) collective-permute-start(f32[32,2048]{1,0:T(8,128)} %bitcast.198), channel_id=1, source_target_pairs={{24,0},{32,8},{40,16},{48,24},{56,32},{64,40},{72,48},{80,56},{88,... | collective-permute-start | bytes 786440 | tf_op jit(solution)/shard_map/ppermute | solution.py:13
  112.3 15.3 %collective-permute-start.11 = (f32[32,2048]{1,0:T(8,128)}, f32[32,2048]{1,0:T(8,128)}, u32[]{:S(2)}, u32[]{:S(2)}) collective-permute-start(f32[32,2048]{1,0:T(8,128)} %bitcast.197), channel_id=1, source_target_pairs={{32,0},{40,8},{48,16},{56,24},{64,32},{72,40},{80,48},{88,56},{96,... | collective-permute-start | bytes 786440 | tf_op jit(solution)/shard_map/ppermute | solution.py:13
  113.6 22.5 %collective-permute-start.9 = (f32[32,2048]{1,0:T(8,128)}, f32[32,2048]{1,0:T(8,128)}, u32[]{:S(2)}, u32[]{:S(2)}) collective-permute-start(f32[32,2048]{1,0:T(8,128)} %bitcast.235), channel_id=1, source_target_pairs={{16,0},{24,8},{32,16},{40,24},{48,32},{56,40},{64,48},{72,56},{80,... | collective-permute-start | bytes 786440 | tf_op jit(solution)/shard_map/ppermute | solution.py:13
  120.8 17.7 %copy-start.1 = (f32[128,16,128]{0,2,1:T(8,128)S(1)}, f32[128,16,128]{0,2,1:T(8,128)}, u32[]{:S(2)}) copy-start(f32[128,16,128]{0,2,1:T(8,128)} %copy.94) | copy-start | bytes 3145732
  138.4 324.9 %all-reduce.5.cloned.1.call-start = ((), (), s32[]{:S(2)}) async-start(), calls=%async_computation.1 | async-start | bytes 524288 | tf_op jit(solution)/shard_map/psum | solution.py:131
  (8 other events, 18.7 us)
Sparse Core Ops, SparseCore 0:
  138.5 228.9 all-reduce.2
  370.2 93.0 all-reduce.4
